TPU v7x, 32 devices: a whole 2x2x4 slice. The times are simulated.
32 devices in a mesh: comp: 4 (over y, core), gx: 2 (over x), gy: 4 (over z).
Axes of the slice: x: 2, y: 2, z: 4, core: 2. Of those that a mesh axis runs over, the one named last changes fastest.
Arguments:
- state: float32 [32, 32, 128, 128], P('comp', 'gx', 'gy'), may hold values from -4 to 4
- levels: int32 [32, 128], P('gx', 'gy'), may hold values from 0 to 128
- reaction: float32 [3, 8, 8], replicated, may hold values from -2 to 2
Outputs:
- new_state: float32 [32, 32, 128, 128], P('comp', 'gx', 'gy')
Inputs may be any that keep to these rules, and one draw needn't show every extreme that they name: `levels`: 0 marks a land column, 128 a column of full depth.
All inputs are finite; a program needn't handle non-finite values.
Results may differ from a plain program's by a relative error of at most 0.00018.
Values sent between devices are 32-bit elements; how exact they have to be, the bound alone decides.
No kernel may reach another device: no remote copies, remote signals or barrier semaphores. Data moves between devices by JAX's collectives and lax.ppermute only.
A program may use at most 64 MiB of HBM per device.

v0:
```python
import jax
import jax.numpy as jnp
from jax import lax
from jax.sharding import PartitionSpec as P

ITERS = 3


time_step = 0.25
lateral_mix = 0.05
vertical_mix = 0.1
pressure_scale = 0.05
thermal_coef = 1.0
haline_coef = 0.8
coriolis_mean = 0.5
coriolis_slope = 0.5


def padded_2(cells, sides, width):
    for axis, dim in sides:
        count = lax.axis_size(axis)
        head = lax.slice_in_dim(cells, 0, width, axis=dim)
        tail = lax.slice_in_dim(cells, cells.shape[dim] - width, cells.shape[dim], axis=dim)
        cells = jnp.concatenate(
            [
                lax.ppermute(tail, axis, [(i, (i + 1) % count) for i in range(count)]),
                cells,
                lax.ppermute(head, axis, [((i + 1) % count, i) for i in range(count)]),
            ],
            axis=dim,
        )
    return cells


def from_root(block, axis, source):
    block = jnp.where(lax.axis_index(axis) == source, block, jnp.zeros_like(block))
    return lax.psum(block, axis)


def along(padded, axis, shift):
    count_x = padded.shape[1] - 4
    count_y = padded.shape[2] - 4
    if axis == 1:
        return padded[:, 2 + shift : 2 + shift + count_x, 2 : 2 + count_y]
    return padded[:, 2 : 2 + count_x, 2 + shift : 2 + shift + count_y]


def centered(padded, axis):
    return (
        8.0 * (along(padded, axis, 1) - along(padded, axis, -1))
        - (along(padded, axis, 2) - along(padded, axis, -2))
    ) / 12.0


def smoothing(padded, axis):
    return (
        along(padded, axis, 2)
        + along(padded, axis, -2)
        - 4.0 * (along(padded, axis, 1) + along(padded, axis, -1))
        + 6.0 * along(padded, axis, 0)
    ) / 12.0


def transport(padded, east, north):
    return (
        east * centered(padded, 1)
        + jnp.abs(east) * smoothing(padded, 1)
        + north * centered(padded, 2)
        + jnp.abs(north) * smoothing(padded, 2)
    )


def lateral(padded):
    return (
        along(padded, 1, 1)
        + along(padded, 1, -1)
        + along(padded, 2, 1)
        + along(padded, 2, -1)
        - 4.0 * along(padded, 1, 0)
    )


def vertical(center):
    column = jnp.pad(center, ((0, 0), (0, 0), (0, 0), (1, 1)))
    return column[..., 2:] + column[..., :-2] - 2.0 * center


def dynamics_step(padded, mask, latitude, accumulate):
    center = padded[:, 2:-2, 2:-2]
    east = center[0]
    north = center[1]
    moving = padded[0:4]
    density = haline_coef * padded[3] - thermal_coef * padded[2]
    pressure = (pressure_scale * accumulate(density))[None]
    tendency = (
        lateral_mix * lateral(moving)
        + vertical_mix * vertical(center[0:4])
        - transport(moving, east, north)
    )
    rotation = (coriolis_mean + coriolis_slope * latitude)[None, :, None]
    push_east = tendency[0] + rotation * north - centered(pressure, 1)[0]
    push_north = tendency[1] - rotation * east - centered(pressure, 2)[0]
    tendency = jnp.stack([push_east, push_north, tendency[2], tendency[3]])
    advanced = center[0:4] + time_step * (1.5 * tendency - 0.5 * center[4:8])
    return jnp.concatenate([advanced * mask, tendency * mask])


def tracer_step(padded, velocity, mask, coupling):
    center = padded[:, 2:-2, 2:-2]
    growth = 2.0 * jax.nn.sigmoid(velocity[2])
    reacting = growth * jnp.einsum(
        "ij,jxyz->ixyz", coupling, center, precision=lax.Precision.HIGHEST
    )
    tendency = (
        lateral_mix * lateral(padded)
        + vertical_mix * vertical(center)
        + reacting
        - transport(padded, velocity[0], velocity[1])
    )
    return (center + time_step * tendency) * mask


def per_device(state, levels, reaction):
    cells_y = state.shape[2]
    depth_count = state.shape[3]
    slot = lax.axis_index("comp")
    row_first = lax.axis_index("gy") * cells_y
    total_rows = cells_y * lax.axis_size("gy")
    depth = lax.broadcasted_iota(jnp.int32, (1, 1, depth_count), 2)
    mask = (depth < levels[:, :, None]).astype(jnp.float32)
    lower = lax.broadcasted_iota(jnp.int32, (depth_count, depth_count), 0)
    higher = lax.broadcasted_iota(jnp.int32, (depth_count, depth_count), 1)
    summing = (lower <= higher).astype(jnp.float32)
    coupling = lax.dynamic_index_in_dim(reaction, jnp.maximum(slot - 1, 0), 0, keepdims=False)

    def accumulate(density):
        return jnp.dot(density, summing, precision=lax.Precision.HIGHEST)

    def global_rows(width):
        return row_first - width + lax.iota(jnp.int32, cells_y + 2 * width)

    def latitude(width):
        rows = global_rows(width)
        return 2.0 * rows.astype(jnp.float32) / float(total_rows - 1) - 1.0

    current = state * mask[None]
    for step in range(ITERS):
        extend_padded = padded_2(current, (("gx", 1), ("gy", 2)), 2)
        inside_rows = global_rows(2)
        region_latitude = latitude(0)

        def run_dynamics(operands):
            return dynamics_step(operands[0], operands[2], region_latitude, accumulate)

        def run_tracers(operands):
            return tracer_step(operands[0], operands[1], operands[2], coupling)

        current = lax.cond(
            slot == 0,
            run_dynamics,
            run_tracers,
            (
                extend_padded
                * ((inside_rows >= 0) & (inside_rows < total_rows)).astype(jnp.float32)[
                    None, None, :, None
                ],
                from_root(current[0:3], "comp", 0),
                mask,
            ),
        )
    return current


def solution(mesh):
    in_specs = (P("comp", "gx", "gy", None), P("gx", "gy"), P())
    out_specs = P("comp", "gx", "gy", None)
    return jax.shard_map(
        per_device, mesh=mesh, in_specs=in_specs, out_specs=out_specs, check_vma=False
    )
```

profile of v0, /device:TPU:20, one launch (start us, length us, event | category | flops | bytes accessed | tf_op | source)
XLA Modules:
  0.0 189.5 jit_solution(14269763152524657210)
XLA Ops:
  6.5 0.8 fusion.99
  7.4 1.9 %broadcast_multiply_fusion = f32[8,16,32,128]{3,2,1,0:T(8,128)S(1)} fusion(f32[8,16,32,128]{3,2,1,0:T(8,128)} %param.9, f32[16,32,128]{2,1,0:T(8,128)S(1)} %fusion.99), kind=kLoop, calls=%fused_computation.174 | loop fusion | flops 524288 | bytes 4456448 | tf_op jit(solution)/shard_map/mul | solution.py:146
  9.4 1.6 collective-permute-start
  10.9 0.5 collective-permute-start.1
  11.5 1.0 slice_select_fusion.2
  12.5 0.6 fusion.100
  13.2 5.5 %collective-permute-done = f32[8,2,32,128]{3,2,1,0:T(8,128)S(1)} collective-permute-done((f32[8,2,32,128]{3,2,1,0:T(8,128)S(1)}, f32[8,2,32,128]{3,2,1,0:T(8,128)S(1)}, u32[]{:S(2)}, u32[]{:S(2)}) %collective-permute-start) | collective-permute-done | bytes 262176 | tf_op jit(solution)/shard_map/ppermute | solution.py:26
  18.6 4.5 %collective-permute-done.1 = f32[8,2,32,128]{3,2,1,0:T(8,128)S(1)} collective-permute-done((f32[8,2,32,128]{3,2,1,0:T(8,128)S(1)}, f32[8,2,32,128]{3,2,1,0:T(8,128)S(1)}, u32[]{:S(2)}, u32[]{:S(2)}) %collective-permute-start.1) | collective-permute-done | bytes 262176 | tf_op jit(solution)/shard_map/ppermute | solution.py:28
  23.1 0.1 pad_maximum_fusion.14
  23.2 1.6 collective-permute-start.2
  24.9 0.4 collective-permute-start.3
  25.3 6.8 %collective-permute-done.2 = f32[8,20,2,128]{3,2,1,0:T(2,128)S(1)} collective-permute-done((f32[8,20,2,128]{3,2,1,0:T(2,128)S(1)}, f32[8,20,2,128]{3,2,1,0:T(2,128)S(1)}, u32[]{:S(2)}, u32[]{:S(2)}) %collective-permute-start.2) | collective-permute-done | bytes 163872 | tf_op jit(solution)/shard_map/ppermute | solution.py:26
  32.1 0.7 copy-done.14
  32.8 2.3 %maximum_multiply_fusion = f32[8,20,36,128]{3,2,1,0:T(8,128)S(1)} fusion(f32[8,20,2,128]{3,2,1,0:T(2,128)} %collective-permute-done.3, f32[8,2,32,128]{3,2,1,0:T(8,128)} %copy-done.7, f32[8,16,32,128]{3,2,1,0:T(8,128)} %copy-done.2, f32[8,2,32,128]{3,2,1,0:T(8,128)} %copy-done.6, f32[8,20,2,128]{3,2,1,0:T(2,128)} %copy-done.14, f32[36]{0:T(128)S(1)} %and_convert_fusion), kind=kLoop, calls=%fused_computation.171 | loop fusion | flops 3686400 | bytes 5898384 | tf_op jit(solution)/shard_map/mul | solution.py:163
  35.1 12.4 %all-reduce.10.cloned.1.call-done = f32[3,16,32,128]{3,2,1,0:T(8,128)} async-done(((f32[3,16,32,128]{3,2,1,0:T(8,128)}), f32[3,16,32,128]{3,2,1,0:T(8,128)}) %all-reduce.10.cloned.1.call-update) | async-done | bytes 786448 | tf_op jit(solution)/shard_map/psum | solution.py:37
  47.5 9.7 %conditional.3 = (f32[8,16,32,128]{3,2,1,0:T(8,128)S(1)}) conditional(s32[]{:T(128)} %convert_element_type.41, (f32[8,20,36,128]{3,2,1,0:T(8,128)S(1)}, f32[3,16,32,128]{3,2,1,0:T(8,128)}, f32[8,8]{1,0:T(8,128)S(1)}, f32[16,32,128]{2,1,0:T(8,128)S(1)}) %tuple.23, (f32[8,20,36,128]{3,2,1,0:T(8,128)S(1)}, f32[32]{0:T(128)S(1)}, f32[128,128]{1,0:T(8,128)}, ...), branch_computations={%region_1.2_spmd, %region_2.3_spmd} | conditional | flops 155859008 | bytes 41029640 | solution.py:158
  47.5 1.3 multiply_bitcast_fusion.4
  48.8 1.7 copy.9
  50.5 0.1 slice.573
  50.6 6.1 %fusion.8 = f32[8,16,32,128]{3,0,2,1:T(8,128)S(1)} fusion(f32[8,16,32,128]{3,0,2,1:T(8,128)S(1)} %slice.573, f32[8,20,36,128]{3,0,2,1:T(8,128)S(1)} %copy.9, f32[16,32,128]{2,1,0:T(8,128)S(1)} %get-tuple-element.65, f32[16,32,128]{2,1,0:T(8,128)S(1)} %get-tuple-element.102, f32[16,32,128]{2,1,0:T(8,128)S(1)} %get-tuple-element.104, ...), kind=kOutput, calls=%fused_computation.10 | convolution fusion | flops 72351744 | bytes 24645632 | tf_op jit(solution)/shard_map/cond/branch_0_fun/ij,jxyz->ixyz/dot_general | solution.py:111
  56.7 0.4 copy.6
  57.2 1.5 collective-permute-start.4
  58.8 0.6 collective-permute-start.5
  59.3 7.2 %collective-permute-done.4 = f32[8,2,32,128]{3,2,1,0:T(8,128)S(1)} collective-permute-done((f32[8,2,32,128]{3,2,1,0:T(8,128)S(1)}, f32[8,2,32,128]{3,2,1,0:T(8,128)S(1)}, u32[]{:S(2)}, u32[]{:S(2)}) %collective-permute-start.4) | collective-permute-done | bytes 262176 | tf_op jit(solution)/shard_map/ppermute | solution.py:26
  66.5 4.0 %collective-permute-done.5 = f32[8,2,32,128]{3,2,1,0:T(8,128)S(1)} collective-permute-done((f32[8,2,32,128]{3,2,1,0:T(8,128)S(1)}, f32[8,2,32,128]{3,2,1,0:T(8,128)S(1)}, u32[]{:S(2)}, u32[]{:S(2)}) %collective-permute-start.5) | collective-permute-done | bytes 262176 | tf_op jit(solution)/shard_map/ppermute | solution.py:28
  70.5 0.1 pad_maximum_fusion.11
  70.6 0.6 copy-done.10
  71.2 1.5 collective-permute-start.6
  72.7 0.5 collective-permute-start.7
  73.2 1.0 slice_select_fusion.1
  74.2 0.0 all-reduce.14.cloned.1.call-start
  74.3 3.7 %collective-permute-done.6 = f32[8,20,2,128]{3,2,1,0:T(2,128)S(1)} collective-permute-done((f32[8,20,2,128]{3,2,1,0:T(2,128)S(1)}, f32[8,20,2,128]{3,2,1,0:T(2,128)S(1)}, u32[]{:S(2)}, u32[]{:S(2)}) %collective-permute-start.6) | collective-permute-done | bytes 163872 | tf_op jit(solution)/shard_map/ppermute | solution.py:26
  78.0 0.7 copy-done.12
  78.7 0.9 collective-permute-done.7
  79.5 2.4 %maximum_multiply_fusion.1 = f32[8,20,36,128]{3,2,1,0:T(8,128)S(1)} fusion(f32[8,20,2,128]{3,2,1,0:T(2,128)} %collective-permute-done.7, f32[8,2,32,128]{3,2,1,0:T(8,128)} %copy-done.10, f32[8,16,32,128]{3,2,1,0:T(8,128)} %copy-done.3, f32[8,2,32,128]{3,2,1,0:T(8,128)} %copy-done.8, f32[8,20,2,128]{3,2,1,0:T(2,128)} %copy-done.12, f32[36]{0:T(128)S(1)} %and_convert_fusion), kind=kLoop, calls=%fused_computation.172 | loop fusion | flops 3686400 | bytes 5898384 | tf_op jit(solution)/shard_map/mul | solution.py:163
  81.9 27.3 %all-reduce.12.cloned.1.call-done = f32[3,16,32,128]{3,2,1,0:T(8,128)} async-done(((f32[3,16,32,128]{3,2,1,0:T(8,128)}), f32[3,16,32,128]{3,2,1,0:T(8,128)}) %all-reduce.12.cloned.1.call-update) | async-done | bytes 786448 | tf_op jit(solution)/shard_map/psum | solution.py:37
  109.2 9.7 %conditional.4 = (f32[8,16,32,128]{3,2,1,0:T(8,128)S(1)}) conditional(s32[]{:T(128)} %convert_element_type.41, (f32[8,20,36,128]{3,2,1,0:T(8,128)S(1)}, f32[3,16,32,128]{3,2,1,0:T(8,128)}, f32[8,8]{1,0:T(8,128)S(1)}, f32[16,32,128]{2,1,0:T(8,128)S(1)}) %tuple.25, (f32[8,20,36,128]{3,2,1,0:T(8,128)S(1)}, f32[32]{0:T(128)S(1)}, f32[128,128]{1,0:T(8,128)}, ...), branch_computations={%region_4.5_spmd, %region_5.6_spmd} | conditional | flops 155859008 | bytes 41029640 | solution.py:158
  109.2 1.3 multiply_bitcast_fusion.13
  110.5 1.7 copy.10
  112.2 0.1 slice.593
  112.4 6.1 %fusion.41 = f32[8,16,32,128]{3,0,2,1:T(8,128)S(1)} fusion(f32[8,16,32,128]{3,0,2,1:T(8,128)S(1)} %slice.593, f32[8,20,36,128]{3,0,2,1:T(8,128)S(1)} %copy.10, f32[16,32,128]{2,1,0:T(8,128)S(1)} %get-tuple-element.73, f32[16,32,128]{2,1,0:T(8,128)S(1)} %get-tuple-element.115, f32[16,32,128]{2,1,0:T(8,128)S(1)} %get-tuple-element.117, ...), kind=kOutput, calls=%fused_computation.67 | convolution fusion | flops 72351744 | bytes 24645632 | tf_op jit(solution)/shard_map/cond/branch_0_fun/ij,jxyz->ixyz/dot_general | solution.py:111
  118.5 0.4 copy.7
  119.0 1.5 collective-permute-start.8
  120.5 0.6 collective-permute-start.9
  121.1 7.2 %collective-permute-done.8 = f32[8,2,32,128]{3,2,1,0:T(8,128)S(1)} collective-permute-done((f32[8,2,32,128]{3,2,1,0:T(8,128)S(1)}, f32[8,2,32,128]{3,2,1,0:T(8,128)S(1)}, u32[]{:S(2)}, u32[]{:S(2)}) %collective-permute-start.8) | collective-permute-done | bytes 262176 | tf_op jit(solution)/shard_map/ppermute | solution.py:26
  128.2 4.0 %collective-permute-done.9 = f32[8,2,32,128]{3,2,1,0:T(8,128)S(1)} collective-permute-done((f32[8,2,32,128]{3,2,1,0:T(8,128)S(1)}, f32[8,2,32,128]{3,2,1,0:T(8,128)S(1)}, u32[]{:S(2)}, u32[]{:S(2)}) %collective-permute-start.9) | collective-permute-done | bytes 262176 | tf_op jit(solution)/shard_map/ppermute | solution.py:28
  132.3 0.1 pad_maximum_fusion.8
  132.4 0.6 copy-done.11
  133.0 1.5 collective-permute-start.10
  134.5 0.5 collective-permute-start.11
  135.0 1.0 slice_select_fusion
  136.0 3.8 %collective-permute-done.10 = f32[8,20,2,128]{3,2,1,0:T(2,128)S(1)} collective-permute-done((f32[8,20,2,128]{3,2,1,0:T(2,128)S(1)}, f32[8,20,2,128]{3,2,1,0:T(2,128)S(1)}, u32[]{:S(2)}, u32[]{:S(2)}) %collective-permute-start.10) | collective-permute-done | bytes 163872 | tf_op jit(solution)/shard_map/ppermute | solution.py:26
  139.8 0.7 copy-done.13
  140.4 0.9 collective-permute-done.11
  141.3 2.4 %maximum_multiply_fusion.2 = f32[8,20,36,128]{3,2,1,0:T(8,128)S(1)} fusion(f32[8,20,2,128]{3,2,1,0:T(2,128)} %collective-permute-done.11, f32[8,2,32,128]{3,2,1,0:T(8,128)} %copy-done.11, f32[8,16,32,128]{3,2,1,0:T(8,128)} %copy-done.4, f32[8,2,32,128]{3,2,1,0:T(8,128)} %copy-done.9, f32[8,20,2,128]{3,2,1,0:T(2,128)} %copy-done.13, f32[36]{0:T(128)S(1)} %and_convert_fusion), kind=kLoop, calls=%fused_computation.173 | loop fusion | flops 3686400 | bytes 5898384 | tf_op jit(solution)/shard_map/mul | solution.py:163
  143.7 27.3 %all-reduce.14.cloned.1.call-done = f32[3,16,32,128]{3,2,1,0:T(8,128)} async-done(((f32[3,16,32,128]{3,2,1,0:T(8,128)}), f32[3,16,32,128]{3,2,1,0:T(8,128)}) %all-reduce.14.cloned.1.call-update) | async-done | bytes 786448 | tf_op jit(solution)/shard_map/psum | solution.py:37
  171.0 9.9 %conditional.5 = (f32[8,16,32,128]{3,2,1,0:T(8,128)S(1)}) conditional(s32[]{:T(128)} %convert_element_type.41, (f32[8,20,36,128]{3,2,1,0:T(8,128)S(1)}, f32[3,16,32,128]{3,2,1,0:T(8,128)}, f32[8,8]{1,0:T(8,128)S(1)}, f32[16,32,128]{2,1,0:T(8,128)S(1)}) %tuple.27, (f32[8,20,36,128]{3,2,1,0:T(8,128)S(1)}, f32[32]{0:T(128)S(1)}, f32[128,128]{1,0:T(8,128)}, ...), branch_computations={%region_7.8_spmd, %region_8.9_spmd} | conditional | flops 155859008 | bytes 41029640 | solution.py:158
  171.0 1.3 multiply_bitcast_fusion.22
  172.3 1.7 copy.11
  174.0 0.1 slice.613
  174.1 6.1 %fusion.74 = f32[8,16,32,128]{3,0,2,1:T(8,128)S(1)} fusion(f32[8,16,32,128]{3,0,2,1:T(8,128)S(1)} %slice.613, f32[8,20,36,128]{3,0,2,1:T(8,128)S(1)} %copy.11, f32[16,32,128]{2,1,0:T(8,128)S(1)} %get-tuple-element.81, f32[16,32,128]{2,1,0:T(8,128)S(1)} %get-tuple-element.128, f32[16,32,128]{2,1,0:T(8,128)S(1)} %get-tuple-element.130, ...), kind=kOutput, calls=%fused_computation.124 | convolution fusion | flops 72351744 | bytes 24645632 | tf_op jit(solution)/shard_map/cond/branch_0_fun/ij,jxyz->ixyz/dot_general | solution.py:111
  180.3 0.4 copy.8
  180.9 1.3 copy-done.5
  182.2 0.7 copy-done.1
  (35 shorter events, 0.3 us)
Async XLA Ops:
  6.5 6.0 %copy-start = (f32[3,8,8]{2,1,0:T(8,128)S(1)}, f32[3,8,8]{2,1,0:T(8,128)}, u32[]{:S(2)}) copy-start(f32[3,8,8]{2,1,0:T(8,128)} %param.11) | copy-start | bytes 2308
  6.5 40.9 %all-reduce.10.cloned.1.call-start = ((), (), s32[]{:S(2)}) async-start(), calls=%async_computation | async-start | bytes 1572864 | tf_op jit(solution)/shard_map/psum | solution.py:37
  9.3 13.9 %copy-start.2 = (f32[8,16,32,128]{3,2,1,0:T(8,128)}, f32[8,16,32,128]{3,2,1,0:T(8,128)S(1)}, u32[]{:S(2)}) copy-start(f32[8,16,32,128]{3,2,1,0:T(8,128)S(1)} %broadcast_multiply_fusion) | copy-start | bytes 6291460
  9.4 9.2 %collective-permute-start = (f32[8,2,32,128]{3,2,1,0:T(8,128)S(1)}, f32[8,2,32,128]{3,2,1,0:T(8,128)S(1)}, u32[]{:S(2)}, u32[]{:S(2)}) collective-permute-start(f32[8,2,32,128]{3,2,1,0:T(8,128)S(1)} %get-tuple-element.149), channel_id=1, source_target_pairs={{0,4},{4,0},{1,5},{5,1},{2,6},{6,2},{3,7},{7,3},{8,12},{12,8},{9,1... | collective-permute-start | bytes 786440 | tf_op jit(solution)/shard_map/ppermute | solution.py:26
  10.9 12.2 %collective-permute-start.1 = (f32[8,2,32,128]{3,2,1,0:T(8,128)S(1)}, f32[8,2,32,128]{3,2,1,0:T(8,128)S(1)}, u32[]{:S(2)}, u32[]{:S(2)}) collective-permute-start(f32[8,2,32,128]{3,2,1,0:T(8,128)S(1)} %get-tuple-element.150), channel_id=1, source_target_pairs={{4,0},{0,4},{5,1},{1,5},{6,2},{2,6},{7,3},{3,7},{12,8},{8,12},{13,... | collective-permute-start | bytes 786440 | tf_op jit(solution)/shard_map/ppermute | solution.py:28
  12.4 96.8 %all-reduce.12.cloned.1.call-start = ((), (), s32[]{:S(2)}) async-start(), calls=%async_computation.1 | async-start | bytes 1572864 | tf_op jit(solution)/shard_map/psum | solution.py:37
  18.6 13.5 %copy-start.6 = (f32[8,2,32,128]{3,2,1,0:T(8,128)}, f32[8,2,32,128]{3,2,1,0:T(8,128)S(1)}, u32[]{:S(2)}) copy-start(f32[8,2,32,128]{3,2,1,0:T(8,128)S(1)} %collective-permute-done) | copy-start | bytes 786436
  23.1 9.0 %copy-start.7 = (f32[8,2,32,128]{3,2,1,0:T(8,128)}, f32[8,2,32,128]{3,2,1,0:T(8,128)S(1)}, u32[]{:S(2)}) copy-start(f32[8,2,32,128]{3,2,1,0:T(8,128)S(1)} %collective-permute-done.1) | copy-start | bytes 786436
  23.2 8.9 %collective-permute-start.2 = (f32[8,20,2,128]{3,2,1,0:T(2,128)S(1)}, f32[8,20,2,128]{3,2,1,0:T(2,128)S(1)}, u32[]{:S(2)}, u32[]{:S(2)}) collective-permute-start(f32[8,20,2,128]{3,2,1,0:T(2,128)S(1)} %get-tuple-element.143), channel_id=1, source_target_pairs={{0,1},{1,2},{2,3},{3,0},{4,5},{5,6},{6,7},{7,4},{8,9},{9,10},{10,1... | collective-permute-start | bytes 491528 | tf_op jit(solution)/shard_map/ppermute | solution.py:26
  24.9 7.9 %collective-permute-start.3 = (f32[8,20,2,128]{3,2,1,0:T(2,128)S(1)}, f32[8,20,2,128]{3,2,1,0:T(2,128)}, u32[]{:S(2)}, u32[]{:S(2)}) collective-permute-start(f32[8,20,2,128]{3,2,1,0:T(2,128)S(1)} %get-tuple-element.144), channel_id=1, source_target_pairs={{1,0},{2,1},{3,2},{0,3},{5,4},{6,5},{7,6},{4,7},{9,8},{10,9},{11,1... | collective-permute-start | bytes 491528 | tf_op jit(solution)/shard_map/ppermute | solution.py:28
  32.1 0.7 copy-start.14
  57.2 17.0 %copy-start.3 = (f32[8,16,32,128]{3,2,1,0:T(8,128)}, f32[8,16,32,128]{3,2,1,0:T(8,128)S(1)}, u32[]{:S(2)}) copy-start(f32[8,16,32,128]{3,2,1,0:T(8,128)S(1)} %get-tuple-element.153) | copy-start | bytes 6291460
  57.2 9.2 %collective-permute-start.4 = (f32[8,2,32,128]{3,2,1,0:T(8,128)S(1)}, f32[8,2,32,128]{3,2,1,0:T(8,128)S(1)}, u32[]{:S(2)}, u32[]{:S(2)}) collective-permute-start(f32[8,2,32,128]{3,2,1,0:T(8,128)S(1)} %get-tuple-element.147), channel_id=1, source_target_pairs={{0,4},{4,0},{1,5},{5,1},{2,6},{6,2},{3,7},{7,3},{8,12},{12,8},{9,1... | collective-permute-start | bytes 786440 | tf_op jit(solution)/shard_map/ppermute | solution.py:26
  58.8 11.7 %collective-permute-start.5 = (f32[8,2,32,128]{3,2,1,0:T(8,128)S(1)}, f32[8,2,32,128]{3,2,1,0:T(8,128)S(1)}, u32[]{:S(2)}, u32[]{:S(2)}) collective-permute-start(f32[8,2,32,128]{3,2,1,0:T(8,128)S(1)} %get-tuple-element.148), channel_id=1, source_target_pairs={{4,0},{0,4},{5,1},{1,5},{6,2},{2,6},{7,3},{3,7},{12,8},{8,12},{13,... | collective-permute-start | bytes 786440 | tf_op jit(solution)/shard_map/ppermute | solution.py:28
  66.5 4.0 %copy-start.8 = (f32[8,2,32,128]{3,2,1,0:T(8,128)}, f32[8,2,32,128]{3,2,1,0:T(8,128)S(1)}, u32[]{:S(2)}) copy-start(f32[8,2,32,128]{3,2,1,0:T(8,128)S(1)} %collective-permute-done.4) | copy-start | bytes 786436
  70.5 0.7 copy-start.10
  71.2 6.8 %collective-permute-start.6 = (f32[8,20,2,128]{3,2,1,0:T(2,128)S(1)}, f32[8,20,2,128]{3,2,1,0:T(2,128)S(1)}, u32[]{:S(2)}, u32[]{:S(2)}) collective-permute-start(f32[8,20,2,128]{3,2,1,0:T(2,128)S(1)} %get-tuple-element.141), channel_id=1, source_target_pairs={{0,1},{1,2},{2,3},{3,0},{4,5},{5,6},{6,7},{7,4},{8,9},{9,10},{10,1... | collective-permute-start | bytes 491528 | tf_op jit(solution)/shard_map/ppermute | solution.py:26
  72.7 6.8 %collective-permute-start.7 = (f32[8,20,2,128]{3,2,1,0:T(2,128)S(1)}, f32[8,20,2,128]{3,2,1,0:T(2,128)}, u32[]{:S(2)}, u32[]{:S(2)}) collective-permute-start(f32[8,20,2,128]{3,2,1,0:T(2,128)S(1)} %get-tuple-element.142), channel_id=1, source_target_pairs={{1,0},{2,1},{3,2},{0,3},{5,4},{6,5},{7,6},{4,7},{9,8},{10,9},{11,1... | collective-permute-start | bytes 491528 | tf_op jit(solution)/shard_map/ppermute | solution.py:28
  74.2 96.7 %all-reduce.14.cloned.1.call-start = ((), (), s32[]{:S(2)}) async-start(), calls=%async_computation.2 | async-start | bytes 1572864 | tf_op jit(solution)/shard_map/psum | solution.py:37
  78.0 0.7 copy-start.12
  118.9 17.0 %copy-start.4 = (f32[8,16,32,128]{3,2,1,0:T(8,128)}, f32[8,16,32,128]{3,2,1,0:T(8,128)S(1)}, u32[]{:S(2)}) copy-start(f32[8,16,32,128]{3,2,1,0:T(8,128)S(1)} %get-tuple-element.154) | copy-start | bytes 6291460
  119.0 9.2 %collective-permute-start.8 = (f32[8,2,32,128]{3,2,1,0:T(8,128)S(1)}, f32[8,2,32,128]{3,2,1,0:T(8,128)S(1)}, u32[]{:S(2)}, u32[]{:S(2)}) collective-permute-start(f32[8,2,32,128]{3,2,1,0:T(8,128)S(1)} %get-tuple-element.145), channel_id=1, source_target_pairs={{0,4},{4,0},{1,5},{5,1},{2,6},{6,2},{3,7},{7,3},{8,12},{12,8},{9,1... | collective-permute-start | bytes 786440 | tf_op jit(solution)/shard_map/ppermute | solution.py:26
  120.5 11.7 %collective-permute-start.9 = (f32[8,2,32,128]{3,2,1,0:T(8,128)S(1)}, f32[8,2,32,128]{3,2,1,0:T(8,128)S(1)}, u32[]{:S(2)}, u32[]{:S(2)}) collective-permute-start(f32[8,2,32,128]{3,2,1,0:T(8,128)S(1)} %get-tuple-element.146), channel_id=1, source_target_pairs={{4,0},{0,4},{5,1},{1,5},{6,2},{2,6},{7,3},{3,7},{12,8},{8,12},{13,... | collective-permute-start | bytes 786440 | tf_op jit(solution)/shard_map/ppermute | solution.py:28
  128.2 4.0 %copy-start.9 = (f32[8,2,32,128]{3,2,1,0:T(8,128)}, f32[8,2,32,128]{3,2,1,0:T(8,128)S(1)}, u32[]{:S(2)}) copy-start(f32[8,2,32,128]{3,2,1,0:T(8,128)S(1)} %collective-permute-done.8) | copy-start | bytes 786436
  132.3 0.7 copy-start.11
  133.0 6.8 %collective-permute-start.10 = (f32[8,20,2,128]{3,2,1,0:T(2,128)S(1)}, f32[8,20,2,128]{3,2,1,0:T(2,128)S(1)}, u32[]{:S(2)}, u32[]{:S(2)}) collective-permute-start(f32[8,20,2,128]{3,2,1,0:T(2,128)S(1)} %get-tuple-element.139), channel_id=1, source_target_pairs={{0,1},{1,2},{2,3},{3,0},{4,5},{5,6},{6,7},{7,4},{8,9},{9,10},{10,1... | collective-permute-start | bytes 491528 | tf_op jit(solution)/shard_map/ppermute | solution.py:26
  134.5 6.8 %collective-permute-start.11 = (f32[8,20,2,128]{3,2,1,0:T(2,128)S(1)}, f32[8,20,2,128]{3,2,1,0:T(2,128)}, u32[]{:S(2)}, u32[]{:S(2)}) collective-permute-start(f32[8,20,2,128]{3,2,1,0:T(2,128)S(1)} %get-tuple-element.140), channel_id=1, source_target_pairs={{1,0},{2,1},{3,2},{0,3},{5,4},{6,5},{7,6},{4,7},{9,8},{10,9},{11,1... | collective-permute-start | bytes 491528 | tf_op jit(solution)/shard_map/ppermute | solution.py:28
  139.8 0.7 copy-start.13
  180.9 1.3 copy-start.5
  182.2 0.7 copy-start.1
Sparse Core Ops, SparseCore 0:
  12.6 34.8 all-reduce.9
  74.4 34.8 all-reduce.11
  136.1 34.8 all-reduce.13
where the time goes:
time: 191 us; the launch traced here: 189 us
  waiting for transfers between devices  115 us (60%)
  matrix products  18.4 us (10%)
  other arithmetic  17.5 us (9%)
  between operations  13.3 us (7%)
  starting transfers between devices  12.5 us (7%)
  local copies, waits for them, and re-layouts  12.1 us (6%)
    psum x3, waiting for transfers between devices, from_root(): return lax.psum(block, axis)  67 us
    ppermute x6, waiting for transfers between devices, padded_2(): lax.ppermute(tail, axis, [(i, (i + 1) % count) for i in range(count)])  34 us
    dot_general x3, matrix products, tracer_step(): jnp.einsum('ij,jxyz->ixyz', coupling, center, precision=lax.Precision.HIG...  18.4 us
    ppermute x6, waiting for transfers between devices, padded_2(): lax.ppermute(head, axis, [((i + 1) % count, i) for i in range(count)])  14.3 us
    ppermute x6, starting transfers between devices, padded_2(): lax.ppermute(tail, axis, [(i, (i + 1) % count) for i in range(count)])  9.22 us
    mul x3, other arithmetic, per_device(): extend_padded * ((inside_rows >= 0) & (inside_rows < total_rows)).astype(...  7.03 us
    unnamed x30, local copies, waits for them, and re-layouts  5.23 us
    another operation x3, local copies, waits for them, and re-layouts  5.13 us
  transfers between devices with their start and end apart: 15, of which 14 were waited for; matrix products, arithmetic and copies ran while one was open for 6% of the time, Pallas kernels for 0%

commit v1 on v0

v1 whole, which is shorter than its diff:
```python
import functools

import jax
import jax.numpy as jnp
from jax import lax
from jax.experimental import pallas as pl
from jax.experimental.pallas import tpu as pltpu
from jax.sharding import PartitionSpec as P

ITERS = 3

time_step = 0.25
lateral_mix = 0.05
vertical_mix = 0.1
pressure_scale = 0.05
thermal_coef = 1.0
haline_coef = 0.8
coriolis_mean = 0.5
coriolis_slope = 0.5

TOP = 8


def padded_copy(pad, q, recv_x, recv_a, recv_b, gy, fields):
    nx, ny = q.shape[1], q.shape[2]
    even = lax.rem(gy, 2) == 0

    @pl.loop(0, fields)
    def _(f):
        for side, first in ((0, 0), (1, nx + 2)):
            for c in range(2):
                pad[f, first + c, TOP : TOP + ny, :] = recv_x[side, f, c]

        @pl.loop(0, nx)
        def _(x):
            pad[f, x + 2, TOP : TOP + ny, :] = q[f, x]

    def rows(high, low):
        @pl.loop(0, fields)
        def _(f):
            for x in range(nx):
                pad[f, x + 2, TOP + ny : TOP + ny + 2, :] = high[f, x]
                pad[f, x + 2, TOP - 2 : TOP, :] = low[f, x]

    @pl.when(even)
    def _():
        rows(recv_a, recv_b)

    @pl.when(jnp.logical_not(even))
    def _():
        rows(recv_b, recv_a)


def send_edges(q, send_x, send_a, send_b, gy, fields):
    nx, ny = q.shape[1], q.shape[2]
    even = lax.rem(gy, 2) == 0

    @pl.loop(0, fields)
    def _(f):
        for side, first in ((0, nx - 2), (1, 0)):
            for c in range(2):
                send_x[side, f, c] = q[f, first + c]

    def rows(high, low):
        @pl.loop(0, fields)
        def _(f):
            for x in range(nx):
                high[f, x] = q[f, x, ny - 2 : ny, :]
                low[f, x] = q[f, x, 0:2, :]

    @pl.when(even)
    def _():
        rows(send_a, send_b)

    @pl.when(jnp.logical_not(even))
    def _():
        rows(send_b, send_a)


def stencil_weights(east, north, scale):
    out = []
    for a in (east, north):
        size = jnp.abs(a)
        mix = scale * lateral_mix
        eight = (scale * 8.0 / 12.0) * a
        four = mix + (scale * 4.0 / 12.0) * size
        one = (scale / 12.0) * a
        low = (-scale / 12.0) * size
        out += [low - one, four + eight, four - eight, low + one]
    center = (-4.0 * scale * lateral_mix) - (scale * 0.5) * (jnp.abs(east) + jnp.abs(north))
    return out, center


def neighbours(pad, f, x, r0, rows):
    return [
        pad[f, x, pl.ds(TOP + r0, rows), :],
        pad[f, x + 1, pl.ds(TOP + r0, rows), :],
        pad[f, x + 3, pl.ds(TOP + r0, rows), :],
        pad[f, x + 4, pl.ds(TOP + r0, rows), :],
        pad[f, x + 2, pl.ds(TOP + r0 - 2, rows), :],
        pad[f, x + 2, pl.ds(TOP + r0 - 1, rows), :],
        pad[f, x + 2, pl.ds(TOP + r0 + 1, rows), :],
        pad[f, x + 2, pl.ds(TOP + r0 + 2, rows), :],
    ]


def weighted(weights, values):
    total = None
    for w, v in zip(weights, values):
        term = w * v
        total = term if total is None else total + term
    return total


def vertical_weights(rows, depth, scale):
    k = lax.broadcasted_iota(jnp.int32, (rows, depth), 1)
    zero = jnp.zeros((rows, depth), jnp.float32)
    above = jnp.where(k == 0, zero, scale)
    below = jnp.where(k == depth - 1, zero, scale)
    return above, below


def tracer_update(pad, mask, vel, coupling, new, rows):
    nx, ny, depth = mask.shape
    scale = time_step
    above, below = vertical_weights(rows, depth, scale * vertical_mix)
    fields = new.shape[0]
    for r0 in range(0, ny, rows):

        @pl.loop(0, nx)
        def _(x):
            here = [pad[f, x + 2, pl.ds(TOP + r0, rows), :] for f in range(fields)]
            for i in range(fields):
                total = coupling[i, 0] * here[0]
                for j in range(1, fields):
                    total = total + coupling[i, j] * here[j]
                new[i, x, pl.ds(r0, rows), :] = total

        @pl.loop(0, nx)
        def _(x):
            east = vel[0, x, pl.ds(r0, rows), :]
            north = vel[1, x, pl.ds(r0, rows), :]
            growth = (2.0 * scale) * jax.nn.sigmoid(vel[2, x, pl.ds(r0, rows), :])
            sea = mask[x, pl.ds(r0, rows), :]
            weights, center = stencil_weights(east, north, scale)
            center = center + (1.0 - 2.0 * scale * vertical_mix)
            for f in range(fields):
                q = pad[f, x + 2, pl.ds(TOP + r0, rows), :]
                total = weighted(weights, neighbours(pad, f, x, r0, rows))
                total = total + center * q
                total = total + above * pltpu.roll(q, 1, 1)
                total = total + below * pltpu.roll(q, depth - 1, 1)
                total = total + growth * new[f, x, pl.ds(r0, rows), :]
                new[f, x, pl.ds(r0, rows), :] = sea * total


def dynamics_update(pad, q, mask, slope, new, gy, total_rows, rows):
    nx, ny, depth = mask.shape
    rho = 4

    @pl.loop(0, nx + 4)
    def _(x):
        pad[rho, x] = haline_coef * pad[3, x] - thermal_coef * pad[2, x]

    @pl.loop(0, nx)
    def _(x):
        n = neighbours(pad, rho, x, 0, ny)
        first = pressure_scale * 8.0 / 12.0
        second = pressure_scale / 12.0
        slope[0, x] = first * (n[2] - n[1]) - second * (n[3] - n[0])
        slope[1, x] = first * (n[6] - n[5]) - second * (n[7] - n[4])

    lower = lax.broadcasted_iota(jnp.int32, (depth, depth), 0)
    higher = lax.broadcasted_iota(jnp.int32, (depth, depth), 1)
    summing = (lower <= higher).astype(jnp.float32)
    for axis in range(2):

        @pl.loop(0, nx, step=4)
        def _(x):
            part = slope[axis, pl.ds(x, 4)].reshape(4 * ny, depth)
            summed = jnp.dot(
                part,
                summing,
                precision=lax.Precision.HIGHEST,
                preferred_element_type=jnp.float32,
            )
            slope[axis, pl.ds(x, 4)] = summed.reshape(4, ny, depth)

    above, below = vertical_weights(rows, depth, vertical_mix)
    for r0 in range(0, ny, rows):
        row = gy * ny + r0 + lax.broadcasted_iota(jnp.int32, (rows, depth), 0)
        latitude = row.astype(jnp.float32) * (2.0 / float(total_rows - 1)) - 1.0
        rotation = coriolis_mean + coriolis_slope * latitude

        @pl.loop(0, nx)
        def _(x):
            here = [pad[f, x + 2, pl.ds(TOP + r0, rows), :] for f in range(4)]
            sea = mask[x, pl.ds(r0, rows), :]
            weights, center = stencil_weights(here[0], here[1], 1.0)
            center = center - 2.0 * vertical_mix
            for f in range(4):
                total = weighted(weights, neighbours(pad, f, x, r0, rows))
                total = total + center * here[f]
                total = total + above * pltpu.roll(here[f], 1, 1)
                total = total + below * pltpu.roll(here[f], depth - 1, 1)
                if f == 0:
                    total = total + rotation * here[1] - slope[0, x, pl.ds(r0, rows), :]
                if f == 1:
                    total = total - rotation * here[0] - slope[1, x, pl.ds(r0, rows), :]
                previous = q[4 + f, x, pl.ds(r0, rows), :]
                moved = here[f] + (1.5 * time_step) * total - (0.5 * time_step) * previous
                new[f, x, pl.ds(r0, rows), :] = sea * moved
                new[4 + f, x, pl.ds(r0, rows), :] = sea * total


def step_kernel(last, total_rows, q, mask, recv_x, recv_a, recv_b, kept, came, coupling, *rest):
    if last:
        new, pad, slope, vel = rest
    else:
        new, send_x, send_a, send_b, speed, pad, slope, vel = rest
    slot = lax.axis_index("comp")
    gy = lax.axis_index("gy")
    fields = q.shape[0]

    @pl.when(slot == 0)
    def _():
        padded_copy(pad, q, recv_x, recv_a, recv_b, gy, 4)
        dynamics_update(pad, q, mask, slope, new, gy, total_rows, 16)
        if not last:
            speed[...] = new[0:3]

    @pl.when(slot > 0)
    def _():
        padded_copy(pad, q, recv_x, recv_a, recv_b, gy, fields)

        @pl.when(lax.rem(slot, 2) == 0)
        def _():
            vel[...] = kept[...]

        @pl.when(lax.rem(slot, 2) == 1)
        def _():
            vel[...] = came[...]

        tracer_update(pad, mask, vel, coupling, new, 16)

    if not last:
        send_edges(new, send_x, send_a, send_b, gy, fields)


def start_kernel(state, mask, q, send_x, send_a, send_b, speed):
    gy = lax.axis_index("gy")
    fields, nx = state.shape[:2]

    @pl.loop(0, fields)
    def _(f):
        @pl.loop(0, nx)
        def _(x):
            q[f, x] = state[f, x] * mask[x]

    speed[...] = q[0:3]
    send_edges(q, send_x, send_a, send_b, gy, fields)


def vmem_specs(count):
    return [pl.BlockSpec(memory_space=pltpu.VMEM)] * count


PARAMS = pltpu.CompilerParams(vmem_limit_bytes=24 * 1024 * 1024)


def per_device(state, levels, reaction):
    fields, nx, ny, depth = state.shape
    comp_count = lax.axis_size("comp")
    gx_count = lax.axis_size("gx")
    gy_count = lax.axis_size("gy")
    slot = lax.axis_index("comp")
    total_rows = ny * gy_count
    level = lax.broadcasted_iota(jnp.int32, (1, 1, depth), 2)
    mask = (level < levels[:, :, None]).astype(jnp.float32)
    coupling = lax.dynamic_index_in_dim(reaction, jnp.maximum(slot - 1, 0), 0, keepdims=False)

    f32 = functools.partial(jax.ShapeDtypeStruct, dtype=jnp.float32)
    whole = f32((fields, nx, ny, depth))
    sends = [
        f32((2, fields, 2, ny, depth)),
        f32((fields, nx, 2, depth)),
        f32((fields, nx, 2, depth)),
        f32((3, nx, ny, depth)),
    ]

    def exchange_x(send):
        if gx_count == 2:
            return lax.ppermute(send, "gx", [(0, 1), (1, 0)])
        tail = lax.ppermute(send[0], "gx", [(i, (i + 1) % gx_count) for i in range(gx_count)])
        head = lax.ppermute(send[1], "gx", [((i + 1) % gx_count, i) for i in range(gx_count)])
        return jnp.stack([tail, head])

    def exchange_y(send, first):
        pairs = []
        for i in range(first, gy_count - 1, 2):
            pairs += [(i, i + 1), (i + 1, i)]
        return lax.ppermute(send, "gy", pairs)

    def spread(speed):
        hop = 1
        while hop * 2 < comp_count:
            hop *= 2
        kept, came = speed, speed
        while hop >= 1:
            came = lax.ppermute(
                kept, "comp", [(i, i + hop) for i in range(0, comp_count - hop, 2 * hop)]
            )
            if hop > 1:
                kept = jnp.where(lax.rem(slot, 2 * hop) == 0, kept, came)
            hop //= 2
        return kept, came

    q, send_x, send_a, send_b, speed = pl.pallas_call(
        start_kernel,
        out_shape=[whole] + sends,
        in_specs=vmem_specs(2),
        out_specs=vmem_specs(5),
        compiler_params=PARAMS,
        name="start",
    )(state, mask)
    for step in range(ITERS):
        last = step == ITERS - 1
        kept, came = spread(speed)
        recv_x = exchange_x(send_x)
        recv_a = exchange_y(send_a, 0)
        recv_b = exchange_y(send_b, 1)
        out = pl.pallas_call(
            functools.partial(step_kernel, last, total_rows),
            out_shape=[whole] if last else [whole] + sends,
            in_specs=vmem_specs(7) + [pl.BlockSpec(memory_space=pltpu.SMEM)],
            out_specs=vmem_specs(1 if last else 5),
            scratch_shapes=[
                pltpu.VMEM((fields, nx + 4, ny + 16, depth), jnp.float32),
                pltpu.VMEM((2, nx, ny, depth), jnp.float32),
                pltpu.VMEM((3, nx, ny, depth), jnp.float32),
            ],
            compiler_params=PARAMS,
            name="step",
        )(q, mask, recv_x, recv_a, recv_b, kept, came, coupling)
        if last:
            (q,) = out
        else:
            q, send_x, send_a, send_b, speed = out
    return q


def solution(mesh):
    in_specs = (P("comp", "gx", "gy", None), P("gx", "gy"), P())
    out_specs = P("comp", "gx", "gy", None)
    return jax.shard_map(
        per_device, mesh=mesh, in_specs=in_specs, out_specs=out_specs, check_vma=False
    )
```

time: 191 us -> 104 us (0.54)
  waiting for transfers between devices: 115 us -> 52.6 us
  Pallas kernels: 0 us -> 24.6 us
  matrix products: 18.4 us -> 0 us
  other arithmetic: 17.5 us -> 2.4 us
  between operations: 13.3 us -> 0.16 us
  local copies, waits for them, and re-layouts: 12.1 us -> 1.6 us
  starting transfers between devices: 12.5 us -> 22.6 us
    psum x3 -> x0, waiting for transfers between devices: 67 us -> none  [from_root(): return lax.psum(block, axis)]
    pallas_call x0 -> x4, Pallas kernels: none -> 24.6 us  [the longest x3 22.6 us: per_device(): pl.pallas_call(functools.partial(step_kernel, last, total_rows), out_shap...]
    dot_general x3 -> x0, matrix products: 18.4 us -> none  [tracer_step(): jnp.einsum('ij,jxyz->ixyz', coupling, center, precision=lax.Precision.HIG...]
    mul x7 -> x0, other arithmetic: 12.8 us -> none  [the longest x3 7.03 us: per_device(): extend_padded * ((inside_rows >= 0) & (inside_rows < total_rows)).astype(...]
    ppermute x12 -> x15, starting transfers between devices: 12.4 us -> 22.6 us  [the longest x6 10.5 us: exchange_y(): return lax.ppermute(send, 'gy', pairs)]
    another operation x3 -> x0, local copies, waits for them, and re-layouts: 5.13 us -> none
    ppermute x12 -> x15, waiting for transfers between devices: 48.3 us -> 52.6 us  [the longest x6 37.8 us: spread(): lax.ppermute(kept, 'comp', [(i, i + hop) for i in range(0, comp_count - h...]
    unnamed x30 -> x6, local copies, waits for them, and re-layouts: 5.23 us -> 1.59 us
  transfers between devices with their start and end apart: 15 -> 15, of which waited for: 14 -> 9; matrix products, arithmetic and copies ran while one was open for 6% -> 0% of each run, Pallas kernels for 0% -> 0%
where the time goes in v1:
time: 104 us
  waiting for transfers between devices  52.6 us (51%)
  Pallas kernels  24.6 us (24%)
  starting transfers between devices  22.6 us (22%)
  other arithmetic  2.4 us (2%)
  local copies, waits for them, and re-layouts  1.6 us (2%)
    ppermute x6, waiting for transfers between devices, spread(): lax.ppermute(kept, 'comp', [(i, i + hop) for i in range(0, comp_count - h...  37.8 us
    pallas_call x3, Pallas kernels, per_device(): pl.pallas_call(functools.partial(step_kernel, last, total_rows), out_shap...  22.6 us
    ppermute x6, waiting for transfers between devices, exchange_y(): return lax.ppermute(send, 'gy', pairs)  14.8 us
    ppermute x6, starting transfers between devices, exchange_y(): return lax.ppermute(send, 'gy', pairs)  10.5 us
    ppermute x6, starting transfers between devices, spread(): lax.ppermute(kept, 'comp', [(i, i + hop) for i in range(0, comp_count - h...  8.72 us
    ppermute x3, starting transfers between devices, exchange_x(): return lax.ppermute(send, 'gx', [(0, 1), (1, 0)])  3.43 us
  transfers between devices with their start and end apart: 15, of which 9 were waited for; matrix products, arithmetic and copies ran while one was open for 0% of the time, Pallas kernels for 0%

profile of v1, /device:TPU:20, one launch (start us, length us, event | category | flops | bytes accessed | tf_op | source)
XLA Modules:
  0.0 104.0 jit_solution(2606755565895749190)
XLA Ops:
  0.0 0.0 copy-start
  0.0 0.8 fusion.mask
  0.9 0.0 copy-start.1
  0.9 1.6 %copy-done.1 = f32[8,16,32,128]{3,2,1,0:T(8,128)S(1)} copy-done((f32[8,16,32,128]{3,2,1,0:T(8,128)S(1)}, f32[8,16,32,128]{3,2,1,0:T(8,128)}, u32[]{:S(2)}) %copy-start.1) | copy-done | bytes 2097176
  2.4 2.1 %start.1 = (f32[8,16,32,128]{3,2,1,0:T(8,128)S(1)}, f32[2,8,2,32,128]{4,3,2,1,0:T(8,128)}, f32[8,16,2,128]{3,2,1,0:T(2,128)}, f32[8,16,2,128]{3,2,1,0:T(2,128)S(1)}, f32[3,16,32,128]{3,2,1,0:T(8,128)S(1)}) custom-call(f32[8,16,32,128]{3,2,1,0:T(8,128)S(1)} %copy-done.1, f32[16,32,128]{2,1,0:T(8,128)S(1)} %fusion.mask), custom_call_target="tpu_custom_call" | custom-call | tf_op jit(solution)/shard_map/start/pallas_call | solution.py:318
  4.5 0.0 copy-start.2
  4.5 1.3 %collective-permute-start.3 = (f32[3,16,32,128]{3,2,1,0:T(8,128)S(1)}, f32[3,16,32,128]{3,2,1,0:T(8,128)}, u32[]{:S(2)}, u32[]{:S(2)}) collective-permute-start(f32[3,16,32,128]{3,2,1,0:T(8,128)S(1)} %get-tuple-element.24), channel_id=1, source_target_pairs={{0,16},{1,17},{2,18},{3,19},{4,20},{5,21},{6,22},{7,23}} | collective-permute-start | bytes 2359304 | tf_op jit(solution)/shard_map/ppermute | solution.py:310
  5.8 0.0 copy-done.2
  5.8 12.7 %collective-permute-done.3 = f32[3,16,32,128]{3,2,1,0:T(8,128)} collective-permute-done((f32[3,16,32,128]{3,2,1,0:T(8,128)S(1)}, f32[3,16,32,128]{3,2,1,0:T(8,128)}, u32[]{:S(2)}, u32[]{:S(2)}) %collective-permute-start.3) | collective-permute-done | bytes 786464 | tf_op jit(solution)/shard_map/ppermute | solution.py:310
  18.5 1.3 %broadcast_select_fusion.2.kept = f32[3,16,32,128]{3,2,1,0:T(8,128)S(1)} fusion(f32[3,16,32,128]{3,2,1,0:T(8,128)} %copy-done.2, f32[3,16,32,128]{3,2,1,0:T(8,128)} %collective-permute-done.3, pred[]{:T(512)S(6)} %eq.2), kind=kLoop, calls=%fused_computation.2 | loop fusion | flops 196608 | bytes 2359297 | tf_op jit(solution)/shard_map/jit(_where)/select_n | solution.py:314
  19.8 2.2 %collective-permute-start.4 = (f32[3,16,32,128]{3,2,1,0:T(8,128)S(1)}, f32[3,16,32,128]{3,2,1,0:T(8,128)}, u32[]{:S(2)}, u32[]{:S(2)}) collective-permute-start(f32[3,16,32,128]{3,2,1,0:T(8,128)S(1)} %broadcast_select_fusion.2.kept), channel_id=1, source_target_pairs={{0,8},{16,24},{1,9},{17,25},{2,10},{18,26},{3,11},{19,27},{4,12},{... | collective-permute-start | bytes 2359304 | tf_op jit(solution)/shard_map/ppermute | solution.py:310
  22.0 1.5 %collective-permute-start = (f32[2,8,2,32,128]{4,3,2,1,0:T(8,128)}, f32[2,8,2,32,128]{4,3,2,1,0:T(8,128)}, u32[]{:S(2)}, u32[]{:S(2)}) collective-permute-start(f32[2,8,2,32,128]{4,3,2,1,0:T(8,128)} %get-tuple-element.21), channel_id=1, source_target_pairs={{0,4},{4,0},{1,5},{5,1},{2,6},{6,2},{3,7},{7,3},{8,12},{12,8},{9,1... | collective-permute-start | bytes 1572872 | tf_op jit(solution)/shard_map/ppermute | solution.py:293
  23.5 1.6 %collective-permute-start.1 = (f32[8,16,2,128]{3,2,1,0:T(2,128)}, f32[8,16,2,128]{3,2,1,0:T(2,128)S(1)}, u32[]{:S(2)}, u32[]{:S(2)}) collective-permute-start(f32[8,16,2,128]{3,2,1,0:T(2,128)} %get-tuple-element.22), channel_id=1, source_target_pairs={{0,1},{1,0},{2,3},{3,2},{4,5},{5,4},{6,7},{7,6},{8,9},{9,8},{10,11... | collective-permute-start | bytes 393224 | tf_op jit(solution)/shard_map/ppermute | solution.py:302
  25.0 1.9 %collective-permute-start.2 = (f32[8,16,2,128]{3,2,1,0:T(2,128)S(1)}, f32[8,16,2,128]{3,2,1,0:T(2,128)S(1)}, u32[]{:S(2)}, u32[]{:S(2)}) collective-permute-start(f32[8,16,2,128]{3,2,1,0:T(2,128)S(1)} %get-tuple-element.23), channel_id=1, source_target_pairs={{1,2},{2,1},{5,6},{6,5},{9,10},{10,9},{13,14},{14,13},{17,18},{18,... | collective-permute-start | bytes 393224 | tf_op jit(solution)/shard_map/ppermute | solution.py:302
  26.9 0.0 copy-done
  27.0 1.7 %collective-permute-done.1.recv_a = f32[8,16,2,128]{3,2,1,0:T(2,128)S(1)} collective-permute-done((f32[8,16,2,128]{3,2,1,0:T(2,128)}, f32[8,16,2,128]{3,2,1,0:T(2,128)S(1)}, u32[]{:S(2)}, u32[]{:S(2)}) %collective-permute-start.1) | collective-permute-done | bytes 131104 | tf_op jit(solution)/shard_map/ppermute | solution.py:302
  28.6 3.2 %collective-permute-done.2.recv_b = f32[8,16,2,128]{3,2,1,0:T(2,128)S(1)} collective-permute-done((f32[8,16,2,128]{3,2,1,0:T(2,128)S(1)}, f32[8,16,2,128]{3,2,1,0:T(2,128)S(1)}, u32[]{:S(2)}, u32[]{:S(2)}) %collective-permute-start.2) | collective-permute-done | bytes 131104 | tf_op jit(solution)/shard_map/ppermute | solution.py:302
  31.9 0.0 collective-permute-done.recv_x
  31.9 0.0 collective-permute-done.4.came
  31.9 7.6 %step.3 = (f32[8,16,32,128]{3,2,1,0:T(8,128)S(1)}, f32[2,8,2,32,128]{4,3,2,1,0:T(8,128)S(1)}, f32[8,16,2,128]{3,2,1,0:T(2,128)S(1)}, f32[8,16,2,128]{3,2,1,0:T(2,128)S(1)}, f32[3,16,32,128]{3,2,1,0:T(8,128)S(1)}) custom-call(f32[8,16,32,128]{3,2,1,0:T(8,128)S(1)} %get-tuple-element.20.q, f32[16,32,128]{2,1,0:T(8,128)S(1)} %fusion.mask, ...), custom_call_target="tpu_custom_call" | custom-call | tf_op jit(solution)/shard_map/step/pallas_call | solution.py:332
  39.5 1.3 %collective-permute-start.8 = (f32[3,16,32,128]{3,2,1,0:T(8,128)S(1)}, f32[3,16,32,128]{3,2,1,0:T(8,128)S(1)}, u32[]{:S(2)}, u32[]{:S(2)}) collective-permute-start(f32[3,16,32,128]{3,2,1,0:T(8,128)S(1)} %get-tuple-element.29), channel_id=1, source_target_pairs={{0,16},{1,17},{2,18},{3,19},{4,20},{5,21},{6,22},{7,23}} | collective-permute-start | bytes 2359304 | tf_op jit(solution)/shard_map/ppermute | solution.py:310
  40.8 12.6 %collective-permute-done.8 = f32[3,16,32,128]{3,2,1,0:T(8,128)S(1)} collective-permute-done((f32[3,16,32,128]{3,2,1,0:T(8,128)S(1)}, f32[3,16,32,128]{3,2,1,0:T(8,128)S(1)}, u32[]{:S(2)}, u32[]{:S(2)}) %collective-permute-start.8) | collective-permute-done | bytes 786464 | tf_op jit(solution)/shard_map/ppermute | solution.py:310
  53.4 0.1 broadcast_select_fusion.1.kept
  53.5 1.3 %collective-permute-start.9 = (f32[3,16,32,128]{3,2,1,0:T(8,128)S(1)}, f32[3,16,32,128]{3,2,1,0:T(8,128)S(1)}, u32[]{:S(2)}, u32[]{:S(2)}) collective-permute-start(f32[3,16,32,128]{3,2,1,0:T(8,128)S(1)} %broadcast_select_fusion.1.kept), channel_id=1, source_target_pairs={{0,8},{16,24},{1,9},{17,25},{2,10},{18,26},{3,11},{19,27},{4,12},{... | collective-permute-start | bytes 2359304 | tf_op jit(solution)/shard_map/ppermute | solution.py:310
  54.9 1.1 %collective-permute-start.5 = (f32[2,8,2,32,128]{4,3,2,1,0:T(8,128)S(1)}, f32[2,8,2,32,128]{4,3,2,1,0:T(8,128)S(1)}, u32[]{:S(2)}, u32[]{:S(2)}) collective-permute-start(f32[2,8,2,32,128]{4,3,2,1,0:T(8,128)S(1)} %get-tuple-element.26), channel_id=1, source_target_pairs={{0,4},{4,0},{1,5},{5,1},{2,6},{6,2},{3,7},{7,3},{8,12},{12,8},{9,1... | collective-permute-start | bytes 1572872 | tf_op jit(solution)/shard_map/ppermute | solution.py:293
  56.0 1.6 %collective-permute-start.6 = (f32[8,16,2,128]{3,2,1,0:T(2,128)S(1)}, f32[8,16,2,128]{3,2,1,0:T(2,128)S(1)}, u32[]{:S(2)}, u32[]{:S(2)}) collective-permute-start(f32[8,16,2,128]{3,2,1,0:T(2,128)S(1)} %get-tuple-element.27), channel_id=1, source_target_pairs={{0,1},{1,0},{2,3},{3,2},{4,5},{5,4},{6,7},{7,6},{8,9},{9,8},{10,11... | collective-permute-start | bytes 393224 | tf_op jit(solution)/shard_map/ppermute | solution.py:302
  57.6 1.9 %collective-permute-start.7 = (f32[8,16,2,128]{3,2,1,0:T(2,128)S(1)}, f32[8,16,2,128]{3,2,1,0:T(2,128)S(1)}, u32[]{:S(2)}, u32[]{:S(2)}) collective-permute-start(f32[8,16,2,128]{3,2,1,0:T(2,128)S(1)} %get-tuple-element.28), channel_id=1, source_target_pairs={{1,2},{2,1},{5,6},{6,5},{9,10},{10,9},{13,14},{14,13},{17,18},{18,... | collective-permute-start | bytes 393224 | tf_op jit(solution)/shard_map/ppermute | solution.py:302
  59.5 1.5 %collective-permute-done.6.recv_a = f32[8,16,2,128]{3,2,1,0:T(2,128)S(1)} collective-permute-done((f32[8,16,2,128]{3,2,1,0:T(2,128)S(1)}, f32[8,16,2,128]{3,2,1,0:T(2,128)S(1)}, u32[]{:S(2)}, u32[]{:S(2)}) %collective-permute-start.6) | collective-permute-done | bytes 131104 | tf_op jit(solution)/shard_map/ppermute | solution.py:302
  61.0 3.5 %collective-permute-done.7.recv_b = f32[8,16,2,128]{3,2,1,0:T(2,128)S(1)} collective-permute-done((f32[8,16,2,128]{3,2,1,0:T(2,128)S(1)}, f32[8,16,2,128]{3,2,1,0:T(2,128)S(1)}, u32[]{:S(2)}, u32[]{:S(2)}) %collective-permute-start.7) | collective-permute-done | bytes 131104 | tf_op jit(solution)/shard_map/ppermute | solution.py:302
  64.4 0.0 collective-permute-done.5.recv_x
  64.4 0.0 collective-permute-done.9.came
  64.5 6.9 %step.4 = (f32[8,16,32,128]{3,2,1,0:T(8,128)S(1)}, f32[2,8,2,32,128]{4,3,2,1,0:T(8,128)S(1)}, f32[8,16,2,128]{3,2,1,0:T(2,128)S(1)}, f32[8,16,2,128]{3,2,1,0:T(2,128)S(1)}, f32[3,16,32,128]{3,2,1,0:T(8,128)S(1)}) custom-call(f32[8,16,32,128]{3,2,1,0:T(8,128)S(1)} %get-tuple-element.25.q, f32[16,32,128]{2,1,0:T(8,128)S(1)} %fusion.mask, ...), custom_call_target="tpu_custom_call" | custom-call | tf_op jit(solution)/shard_map/step/pallas_call | solution.py:332
  71.4 1.3 %collective-permute-start.13 = (f32[3,16,32,128]{3,2,1,0:T(8,128)S(1)}, f32[3,16,32,128]{3,2,1,0:T(8,128)S(1)}, u32[]{:S(2)}, u32[]{:S(2)}) collective-permute-start(f32[3,16,32,128]{3,2,1,0:T(8,128)S(1)} %get-tuple-element.34), channel_id=1, source_target_pairs={{0,16},{1,17},{2,18},{3,19},{4,20},{5,21},{6,22},{7,23}} | collective-permute-start | bytes 2359304 | tf_op jit(solution)/shard_map/ppermute | solution.py:310
  72.7 12.6 %collective-permute-done.13 = f32[3,16,32,128]{3,2,1,0:T(8,128)S(1)} collective-permute-done((f32[3,16,32,128]{3,2,1,0:T(8,128)S(1)}, f32[3,16,32,128]{3,2,1,0:T(8,128)S(1)}, u32[]{:S(2)}, u32[]{:S(2)}) %collective-permute-start.13) | collective-permute-done | bytes 786464 | tf_op jit(solution)/shard_map/ppermute | solution.py:310
  85.3 0.1 broadcast_select_fusion.kept
  85.4 1.3 %collective-permute-start.14 = (f32[3,16,32,128]{3,2,1,0:T(8,128)S(1)}, f32[3,16,32,128]{3,2,1,0:T(8,128)S(1)}, u32[]{:S(2)}, u32[]{:S(2)}) collective-permute-start(f32[3,16,32,128]{3,2,1,0:T(8,128)S(1)} %broadcast_select_fusion.kept), channel_id=1, source_target_pairs={{0,8},{16,24},{1,9},{17,25},{2,10},{18,26},{3,11},{19,27},{4,12},{... | collective-permute-start | bytes 2359304 | tf_op jit(solution)/shard_map/ppermute | solution.py:310
  86.7 0.8 collective-permute-start.10
  87.6 1.6 %collective-permute-start.11 = (f32[8,16,2,128]{3,2,1,0:T(2,128)S(1)}, f32[8,16,2,128]{3,2,1,0:T(2,128)S(1)}, u32[]{:S(2)}, u32[]{:S(2)}) collective-permute-start(f32[8,16,2,128]{3,2,1,0:T(2,128)S(1)} %get-tuple-element.32), channel_id=1, source_target_pairs={{0,1},{1,0},{2,3},{3,2},{4,5},{5,4},{6,7},{7,6},{8,9},{9,8},{10,11... | collective-permute-start | bytes 393224 | tf_op jit(solution)/shard_map/ppermute | solution.py:302
  89.1 1.9 %collective-permute-start.12 = (f32[8,16,2,128]{3,2,1,0:T(2,128)S(1)}, f32[8,16,2,128]{3,2,1,0:T(2,128)S(1)}, u32[]{:S(2)}, u32[]{:S(2)}) collective-permute-start(f32[8,16,2,128]{3,2,1,0:T(2,128)S(1)} %get-tuple-element.33), channel_id=1, source_target_pairs={{1,2},{2,1},{5,6},{6,5},{9,10},{10,9},{13,14},{14,13},{17,18},{18,... | collective-permute-start | bytes 393224 | tf_op jit(solution)/shard_map/ppermute | solution.py:302
  91.1 1.5 %collective-permute-done.11.recv_a = f32[8,16,2,128]{3,2,1,0:T(2,128)S(1)} collective-permute-done((f32[8,16,2,128]{3,2,1,0:T(2,128)S(1)}, f32[8,16,2,128]{3,2,1,0:T(2,128)S(1)}, u32[]{:S(2)}, u32[]{:S(2)}) %collective-permute-start.11) | collective-permute-done | bytes 131104 | tf_op jit(solution)/shard_map/ppermute | solution.py:302
  92.5 3.5 %collective-permute-done.12.recv_b = f32[8,16,2,128]{3,2,1,0:T(2,128)S(1)} collective-permute-done((f32[8,16,2,128]{3,2,1,0:T(2,128)S(1)}, f32[8,16,2,128]{3,2,1,0:T(2,128)S(1)}, u32[]{:S(2)}, u32[]{:S(2)}) %collective-permute-start.12) | collective-permute-done | bytes 131104 | tf_op jit(solution)/shard_map/ppermute | solution.py:302
  96.0 0.0 collective-permute-done.10.recv_x
  96.0 0.0 collective-permute-done.14.came
  96.0 8.0 %step.5 = f32[8,16,32,128]{3,2,1,0:T(8,128)} custom-call(f32[8,16,32,128]{3,2,1,0:T(8,128)S(1)} %get-tuple-element.30.q, f32[16,32,128]{2,1,0:T(8,128)S(1)} %fusion.mask, f32[2,8,2,32,128]{4,3,2,1,0:T(8,128)S(1)} %collective-permute-done.10.recv_x, f32[8,16,2,128]{3,2,1,0:T(2,128)S(1)} %collective-permute-done.11.recv_a, ...), custom_call_target="tpu_custom_call" | custom-call | tf_op jit(solution)/shard_map/step/pallas_call | solution.py:332
  (1 shorter events, 0.0 us)
Async XLA Ops:
  0.0 27.0 %copy-start = (f32[3,8,8]{2,1,0:T(8,128)S(1)}, f32[3,8,8]{2,1,0:T(8,128)}, u32[]{:S(2)}) copy-start(f32[3,8,8]{2,1,0:T(8,128)} %param.5) | copy-start | bytes 2308
  0.9 1.6 %copy-start.1 = (f32[8,16,32,128]{3,2,1,0:T(8,128)S(1)}, f32[8,16,32,128]{3,2,1,0:T(8,128)}, u32[]{:S(2)}) copy-start(f32[8,16,32,128]{3,2,1,0:T(8,128)} %state.1) | copy-start | bytes 6291460
  4.5 1.3 %copy-start.2 = (f32[3,16,32,128]{3,2,1,0:T(8,128)}, f32[3,16,32,128]{3,2,1,0:T(8,128)S(1)}, u32[]{:S(2)}) copy-start(f32[3,16,32,128]{3,2,1,0:T(8,128)S(1)} %get-tuple-element.24) | copy-start | bytes 2359300
  4.5 14.0 %collective-permute-start.3 = (f32[3,16,32,128]{3,2,1,0:T(8,128)S(1)}, f32[3,16,32,128]{3,2,1,0:T(8,128)}, u32[]{:S(2)}, u32[]{:S(2)}) collective-permute-start(f32[3,16,32,128]{3,2,1,0:T(8,128)S(1)} %get-tuple-element.24), channel_id=1, source_target_pairs={{0,16},{1,17},{2,18},{3,19},{4,20},{5,21},{6,22},{7,23}} | collective-permute-start | bytes 2359304 | tf_op jit(solution)/shard_map/ppermute | solution.py:310
  19.8 12.1 %collective-permute-start.4 = (f32[3,16,32,128]{3,2,1,0:T(8,128)S(1)}, f32[3,16,32,128]{3,2,1,0:T(8,128)}, u32[]{:S(2)}, u32[]{:S(2)}) collective-permute-start(f32[3,16,32,128]{3,2,1,0:T(8,128)S(1)} %broadcast_select_fusion.2.kept), channel_id=1, source_target_pairs={{0,8},{16,24},{1,9},{17,25},{2,10},{18,26},{3,11},{19,27},{4,12},{... | collective-permute-start | bytes 2359304 | tf_op jit(solution)/shard_map/ppermute | solution.py:310
  22.0 9.9 %collective-permute-start = (f32[2,8,2,32,128]{4,3,2,1,0:T(8,128)}, f32[2,8,2,32,128]{4,3,2,1,0:T(8,128)}, u32[]{:S(2)}, u32[]{:S(2)}) collective-permute-start(f32[2,8,2,32,128]{4,3,2,1,0:T(8,128)} %get-tuple-element.21), channel_id=1, source_target_pairs={{0,4},{4,0},{1,5},{5,1},{2,6},{6,2},{3,7},{7,3},{8,12},{12,8},{9,1... | collective-permute-start | bytes 1572872 | tf_op jit(solution)/shard_map/ppermute | solution.py:293
  23.5 5.2 %collective-permute-start.1 = (f32[8,16,2,128]{3,2,1,0:T(2,128)}, f32[8,16,2,128]{3,2,1,0:T(2,128)S(1)}, u32[]{:S(2)}, u32[]{:S(2)}) collective-permute-start(f32[8,16,2,128]{3,2,1,0:T(2,128)} %get-tuple-element.22), channel_id=1, source_target_pairs={{0,1},{1,0},{2,3},{3,2},{4,5},{5,4},{6,7},{7,6},{8,9},{9,8},{10,11... | collective-permute-start | bytes 393224 | tf_op jit(solution)/shard_map/ppermute | solution.py:302
  25.0 6.8 %collective-permute-start.2 = (f32[8,16,2,128]{3,2,1,0:T(2,128)S(1)}, f32[8,16,2,128]{3,2,1,0:T(2,128)S(1)}, u32[]{:S(2)}, u32[]{:S(2)}) collective-permute-start(f32[8,16,2,128]{3,2,1,0:T(2,128)S(1)} %get-tuple-element.23), channel_id=1, source_target_pairs={{1,2},{2,1},{5,6},{6,5},{9,10},{10,9},{13,14},{14,13},{17,18},{18,... | collective-permute-start | bytes 393224 | tf_op jit(solution)/shard_map/ppermute | solution.py:302
  39.5 13.9 %collective-permute-start.8 = (f32[3,16,32,128]{3,2,1,0:T(8,128)S(1)}, f32[3,16,32,128]{3,2,1,0:T(8,128)S(1)}, u32[]{:S(2)}, u32[]{:S(2)}) collective-permute-start(f32[3,16,32,128]{3,2,1,0:T(8,128)S(1)} %get-tuple-element.29), channel_id=1, source_target_pairs={{0,16},{1,17},{2,18},{3,19},{4,20},{5,21},{6,22},{7,23}} | collective-permute-start | bytes 2359304 | tf_op jit(solution)/shard_map/ppermute | solution.py:310
  53.5 10.9 %collective-permute-start.9 = (f32[3,16,32,128]{3,2,1,0:T(8,128)S(1)}, f32[3,16,32,128]{3,2,1,0:T(8,128)S(1)}, u32[]{:S(2)}, u32[]{:S(2)}) collective-permute-start(f32[3,16,32,128]{3,2,1,0:T(8,128)S(1)} %broadcast_select_fusion.1.kept), channel_id=1, source_target_pairs={{0,8},{16,24},{1,9},{17,25},{2,10},{18,26},{3,11},{19,27},{4,12},{... | collective-permute-start | bytes 2359304 | tf_op jit(solution)/shard_map/ppermute | solution.py:310
  54.9 9.6 %collective-permute-start.5 = (f32[2,8,2,32,128]{4,3,2,1,0:T(8,128)S(1)}, f32[2,8,2,32,128]{4,3,2,1,0:T(8,128)S(1)}, u32[]{:S(2)}, u32[]{:S(2)}) collective-permute-start(f32[2,8,2,32,128]{4,3,2,1,0:T(8,128)S(1)} %get-tuple-element.26), channel_id=1, source_target_pairs={{0,4},{4,0},{1,5},{5,1},{2,6},{6,2},{3,7},{7,3},{8,12},{12,8},{9,1... | collective-permute-start | bytes 1572872 | tf_op jit(solution)/shard_map/ppermute | solution.py:293
  56.0 5.0 %collective-permute-start.6 = (f32[8,16,2,128]{3,2,1,0:T(2,128)S(1)}, f32[8,16,2,128]{3,2,1,0:T(2,128)S(1)}, u32[]{:S(2)}, u32[]{:S(2)}) collective-permute-start(f32[8,16,2,128]{3,2,1,0:T(2,128)S(1)} %get-tuple-element.27), channel_id=1, source_target_pairs={{0,1},{1,0},{2,3},{3,2},{4,5},{5,4},{6,7},{7,6},{8,9},{9,8},{10,11... | collective-permute-start | bytes 393224 | tf_op jit(solution)/shard_map/ppermute | solution.py:302
  57.6 6.8 %collective-permute-start.7 = (f32[8,16,2,128]{3,2,1,0:T(2,128)S(1)}, f32[8,16,2,128]{3,2,1,0:T(2,128)S(1)}, u32[]{:S(2)}, u32[]{:S(2)}) collective-permute-start(f32[8,16,2,128]{3,2,1,0:T(2,128)S(1)} %get-tuple-element.28), channel_id=1, source_target_pairs={{1,2},{2,1},{5,6},{6,5},{9,10},{10,9},{13,14},{14,13},{17,18},{18,... | collective-permute-start | bytes 393224 | tf_op jit(solution)/shard_map/ppermute | solution.py:302
  71.4 13.9 %collective-permute-start.13 = (f32[3,16,32,128]{3,2,1,0:T(8,128)S(1)}, f32[3,16,32,128]{3,2,1,0:T(8,128)S(1)}, u32[]{:S(2)}, u32[]{:S(2)}) collective-permute-start(f32[3,16,32,128]{3,2,1,0:T(8,128)S(1)} %get-tuple-element.34), channel_id=1, source_target_pairs={{0,16},{1,17},{2,18},{3,19},{4,20},{5,21},{6,22},{7,23}} | collective-permute-start | bytes 2359304 | tf_op jit(solution)/shard_map/ppermute | solution.py:310
  85.4 10.6 %collective-permute-start.14 = (f32[3,16,32,128]{3,2,1,0:T(8,128)S(1)}, f32[3,16,32,128]{3,2,1,0:T(8,128)S(1)}, u32[]{:S(2)}, u32[]{:S(2)}) collective-permute-start(f32[3,16,32,128]{3,2,1,0:T(8,128)S(1)} %broadcast_select_fusion.kept), channel_id=1, source_target_pairs={{0,8},{16,24},{1,9},{17,25},{2,10},{18,26},{3,11},{19,27},{4,12},{... | collective-permute-start | bytes 2359304 | tf_op jit(solution)/shard_map/ppermute | solution.py:310
  86.7 9.2 %collective-permute-start.10 = (f32[2,8,2,32,128]{4,3,2,1,0:T(8,128)S(1)}, f32[2,8,2,32,128]{4,3,2,1,0:T(8,128)S(1)}, u32[]{:S(2)}, u32[]{:S(2)}) collective-permute-start(f32[2,8,2,32,128]{4,3,2,1,0:T(8,128)S(1)} %get-tuple-element.31), channel_id=1, source_target_pairs={{0,4},{4,0},{1,5},{5,1},{2,6},{6,2},{3,7},{7,3},{8,12},{12,8},{9,1... | collective-permute-start | bytes 1572872 | tf_op jit(solution)/shard_map/ppermute | solution.py:293
  87.6 5.0 %collective-permute-start.11 = (f32[8,16,2,128]{3,2,1,0:T(2,128)S(1)}, f32[8,16,2,128]{3,2,1,0:T(2,128)S(1)}, u32[]{:S(2)}, u32[]{:S(2)}) collective-permute-start(f32[8,16,2,128]{3,2,1,0:T(2,128)S(1)} %get-tuple-element.32), channel_id=1, source_target_pairs={{0,1},{1,0},{2,3},{3,2},{4,5},{5,4},{6,7},{7,6},{8,9},{9,8},{10,11... | collective-permute-start | bytes 393224 | tf_op jit(solution)/shard_map/ppermute | solution.py:302
  89.1 6.8 %collective-permute-start.12 = (f32[8,16,2,128]{3,2,1,0:T(2,128)S(1)}, f32[8,16,2,128]{3,2,1,0:T(2,128)S(1)}, u32[]{:S(2)}, u32[]{:S(2)}) collective-permute-start(f32[8,16,2,128]{3,2,1,0:T(2,128)S(1)} %get-tuple-element.33), channel_id=1, source_target_pairs={{1,2},{2,1},{5,6},{6,5},{9,10},{10,9},{13,14},{14,13},{17,18},{18,... | collective-permute-start | bytes 393224 | tf_op jit(solution)/shard_map/ppermute | solution.py:302
